TPU v7x, 256 devices: a whole 4x4x8 slice. The times are simulated.
256 devices in a mesh: prompt: 4 (over x), vocab: 64 (over z, y, core).
Axes of the slice: x: 4, y: 4, z: 8, core: 2. Of those that a mesh axis runs over, the one named last changes fastest.
Arguments:
- hidden: bfloat16 [512, 8192], P('prompt')
- head: bfloat16 [8192, 65536], P('prompt', 'vocab')
- gain: float32 [8192], replicated, may hold values from 0.25 to 1.75
- refusal_ids: int32 [512, 16], P('prompt'), may hold values from 0 to 65535, as said below
- refusal_count: int32 [512], P('prompt'), may hold values from 1 to 16
- loss_scale: float32 [512], P('prompt'), may hold values from 8 to 32
Outputs:
- grad_hidden: float32 [512, 8192], P('prompt', 'vocab')
- log_refusal: float32 [512], P('prompt')
Inputs may be any that keep to these rules, and one draw needn't show every extreme that they name: `refusal_ids`: the first refusal_count entries of a prompt's list are distinct ids below 65536; later entries are ignored.
All inputs are finite; a program needn't handle non-finite values.
Results may differ from a plain program's by a relative error of at most 0.0027.
The roundings to bfloat16 on the way count: a program that leaves them out, or rounds other values in their place, can miss the bound.
Values may be sent and summed in bfloat16 or wider, within the bound.
A program may use at most 128 MiB of HBM per device.

v0:
```python
import jax
import jax.numpy as jnp
from jax import lax
from jax.sharding import PartitionSpec as P

epsilon = 1e-05
lowest = -1e30


def shards(hidden, head, gain, refusal_ids, refusal_count, loss_scale):
    row_count, model_width = hidden.shape
    vocab_local = head.shape[1]
    list_length = refusal_ids.shape[1]
    hidden_f = hidden.astype(jnp.float32)
    inverse_rms = lax.rsqrt(jnp.mean(hidden_f * hidden_f, axis=1, keepdims=True) + epsilon)
    normed = (hidden_f * inverse_rms * gain).astype(jnp.bfloat16)
    logits = jnp.dot(
        normed,
        lax.all_gather(head, "prompt", axis=0, tiled=True),
        preferred_element_type=jnp.float32,
    )
    vocab_start = lax.axis_index("vocab") * vocab_local
    shifted_ids = refusal_ids - vocab_start
    in_list = jnp.arange(list_length)[None, :] < refusal_count[:, None]
    is_local = in_list & (shifted_ids >= 0) & (shifted_ids < vocab_local)
    safe_ids = jnp.clip(shifted_ids, 0, vocab_local - 1)
    picked = jnp.take_along_axis(logits, safe_ids, axis=1)
    peak_all = jnp.max(logits, axis=1)
    peak_ref = jnp.max(jnp.where(is_local, picked, lowest), axis=1)
    peak_all, peak_ref = lax.pmax((peak_all, peak_ref), "vocab")
    sum_all = jnp.sum(jnp.exp(logits - peak_all[:, None]), axis=1)
    sum_ref = jnp.sum(jnp.exp(jnp.where(is_local, picked - peak_ref[:, None], lowest)), axis=1)
    sum_all, sum_ref = lax.psum((sum_all, sum_ref), "vocab")
    lse_all = peak_all + jnp.log(sum_all)
    lse_ref = peak_ref + jnp.log(sum_ref)
    log_refusal = lse_ref - lse_all
    member = jnp.any(
        (safe_ids[:, :, None] == jnp.arange(vocab_local)[None, None, :]) & is_local[:, :, None],
        axis=1,
    )
    grad_logits = loss_scale[:, None] * (
        jnp.exp(jnp.where(member, logits - lse_ref[:, None], lowest))
        - jnp.exp(logits - lse_all[:, None])
    )
    grad_b = grad_logits.astype(jnp.bfloat16)
    slice_width = model_width // lax.axis_size("vocab")
    col_start = lax.axis_index("vocab") * slice_width
    grad_full = lax.dot_general(
        grad_b,
        lax.all_gather(head, "prompt", axis=0, tiled=True),
        (((1,), (1,)), ((), ())),
        preferred_element_type=jnp.float32,
    )
    grad_cols = lax.psum_scatter(grad_full, "vocab", scatter_dimension=1, tiled=True)
    normed_cols = lax.dynamic_slice_in_dim(normed, col_start, slice_width, 1).astype(jnp.float32)
    row_term = lax.psum(jnp.sum(grad_cols * normed_cols, axis=1), "vocab")
    hidden_cols = lax.dynamic_slice_in_dim(hidden_f, col_start, slice_width, 1)
    gain_cols = lax.dynamic_slice_in_dim(gain, col_start, slice_width, 0)
    grad_hidden = (
        inverse_rms * gain_cols * grad_cols
        - hidden_cols * (inverse_rms * inverse_rms / model_width) * row_term[:, None]
    )
    return (grad_hidden, log_refusal)


def solution(mesh):
    return jax.shard_map(
        shards,
        mesh=mesh,
        in_specs=(
            P("prompt", None),
            P("prompt", "vocab"),
            P(),
            P("prompt", None),
            P("prompt"),
            P("prompt"),
        ),
        out_specs=(P("prompt", "vocab"), P("prompt")),
        check_vma=False,
    )
```

profile of v0, /device:TPU:1, one launch (start us, length us, event | category | flops | bytes accessed | tf_op | source)
XLA Modules:
  0.0 739.2 jit_solution(6245504685200072266)
XLA Ops:
  7.2 0.7 all-gather.2.cloned.1.call-update
  8.0 0.1 copy.11
  8.1 0.1 reshape.39
  8.2 0.6 copy-done
  8.8 0.5 multiply_reduce_fusion
  9.3 1.9 multiply_convert_fusion
  11.2 159.1 %all-gather.2.cloned.1.call-done = bf16[8192,1024]{1,0:T(8,128)(2,1)} async-done(((bf16[2048,1024]{1,0:T(8,128)(2,1)}), bf16[8192,1024]{1,0:T(8,128)(2,1)}) %all-gather.2.cloned.1.call-update) | async-done | bytes 16777232 | tf_op jit(solution)/shard_map/all_gather | solution.py:19
  170.3 8.8 %fusion.12 = (f32[128]{0:T(128)S(1)}, f32[128,1024]{1,0:T(8,128)S(1)}) fusion(bf16[128,8192]{1,0:T(8,128)(2,1)} %multiply_convert_fusion, bf16[8192,1024]{1,0:T(8,128)(2,1)} %all-gather.2.cloned.1.call-done), kind=kOutput, calls=%fused_computation.30 | convolution fusion | flops 2147614720 | bytes 19399168 | tf_op jit(solution)/shard_map/dot_general | solution.py:17
  179.2 16.6 %gather_fusion = f32[2048]{0:T(1024)S(1)} fusion(f32[128,1024]{1,0:T(8,128)S(1)} %get-tuple-element.16, s32[2048]{0:T(1024)S(1)} %reshape.39), kind=kCustom, calls=%fused_computation | custom fusion | bytes 32768 | tf_op jit(solution)/shard_map/jit(take_along_axis)/gather | solution.py:27
  195.8 0.1 reshape.42
  195.9 0.2 select_reduce_fusion
  196.1 2.4 fusion.1
  198.5 124.6 %all-reduce.1 = (f32[128]{0:T(128)S(1)}, f32[128]{0:T(128)S(1)}) all-reduce(f32[128]{0:T(128)S(1)} %get-tuple-element.15, f32[128]{0:T(128)S(1)} %get-tuple-element.9), channel_id=1, replica_groups=mesh['prompt'=4,'vocab'=64] {'vocab'}, use_global_device_ids=true, to_apply=%region_7.8 | all-reduce | flops 256 | bytes 2048 | tf_op jit(solution)/shard_map/pmax | solution.py:30
  323.1 0.2 exponential_reduce_fusion.1
  323.3 0.2 exponential_reduce_fusion
  323.5 128.4 %all-reduce = (f32[128]{0:T(128)S(1)}, f32[128]{0:T(128)S(1)}) all-reduce(f32[128]{0:T(128)S(1)} %exponential_reduce_fusion, f32[128]{0:T(128)S(1)} %exponential_reduce_fusion.1), channel_id=1, replica_groups=mesh['prompt'=4,'vocab'=64] {'vocab'}, use_global_device_ids=true, to_apply=%region_9.10 | all-reduce | flops 256 | bytes 2048 | tf_op jit(solution)/shard_map/psum | solution.py:33
  452.0 0.5 fusion.10
  452.5 13.4 %fusion.2 = f32[128,8192]{1,0:T(8,128)} fusion(bf16[8192,1024]{1,0:T(8,128)(2,1)} %all-gather.2.cloned.1.call-done, f32[128,1024]{1,0:T(8,128)S(1)} %get-tuple-element.16, pred[128,1024]{1,0:T(8,128)(4,1)S(1)} %fusion.1, f32[128]{0:T(128)S(1)} %get-tuple-element.8, f32[128]{0:T(128)S(1)} %get-tuple-element.7, f32[128]{0:T(128)S(1)} %copy-done.3), kind=kOutput, calls=%fused_computation.8 | convolution fusion | flops 2148270080 | bytes 21628416 | tf_op jit(solution)/shard_map/dot_general | solution.py:48
  466.0 2.3 convert_element_type.12
  468.3 0.1 dynamic_slice.9
  468.4 132.1 %reduce-scatter.2.cloned.1.call-done = f32[128,128]{1,0:T(8,128)} async-done(((f32[128,8192]{1,0:T(8,128)}), f32[128,128]{1,0:T(8,128)}) %reduce-scatter.2.cloned.1.call-update) | async-done | bytes 65552 | tf_op jit(solution)/shard_map/reduce_scatter | solution.py:54
  600.5 0.9 multiply_reduce_fusion.1
  601.5 129.2 %psum.23 = f32[128]{0:T(128)S(1)} all-reduce(f32[128]{0:T(128)S(1)} %multiply_reduce_fusion.1), channel_id=1, replica_groups=mesh['prompt'=4,'vocab'=64] {'vocab'}, use_global_device_ids=true, to_apply=%region_12.13 | all-reduce | flops 128 | bytes 1024 | tf_op jit(solution)/shard_map/psum | solution.py:56
  730.7 1.6 multiply_subtract_fusion
  (14 shorter events, 0.2 us)
Async XLA Ops:
  7.2 0.8 copy-start.2
  7.2 1.6 copy-start
  7.2 2.1 copy-start.1
  7.2 163.1 %all-gather.2.cloned.1.call-start = ((), (), s32[]{:S(2)}) async-start(), calls=%async_computation.1 | async-start | bytes 20971520 | tf_op jit(solution)/shard_map/all_gather | solution.py:19
  7.9 592.6 %reduce-scatter.2.cloned.1.call-start = ((), (), s32[]{:S(2)}) async-start(), calls=%async_computation.2 | async-start | bytes 4259840 | tf_op jit(solution)/shard_map/reduce_scatter | solution.py:54
  179.1 16.8 %copy-start.4 = (s32[128]{0:T(128)S(1)}, s32[128]{0:T(128)}, u32[]{:S(2)}) copy-start(s32[128]{0:T(128)} %param.10) | copy-start | bytes 1540
  179.1 273.4 %copy-start.3 = (f32[128]{0:T(128)S(1)}, f32[128]{0:T(128)}, u32[]{:S(2)}) copy-start(f32[128]{0:T(128)} %param.11) | copy-start | bytes 1540
Sparse Core Ops, SparseCore 0:
  9.8 160.4 all-gather.1
  466.1 134.3 reduce-scatter.1
where the time goes:
time: 739 us
  blocking collectives  382 us (52%)
  waiting for transfers between devices  292 us (40%)
  matrix products  22.3 us (3%)
  local copies, waits for them, and re-layouts  17.6 us (2%)
  between operations  14.2 us (2%)
  other arithmetic  10.9 us (1%)
    all_gather x1, waiting for transfers between devices, shards(): lax.all_gather(head, 'prompt', axis=0, tiled=True)  159 us
    reduce_scatter x1, waiting for transfers between devices, shards(): lax.psum_scatter(grad_full, 'vocab', scatter_dimension=1, tiled=True)  132 us
    psum x1, blocking collectives, shards(): row_term = lax.psum(jnp.sum(grad_cols * normed_cols, axis=1), 'vocab')  129 us
    psum x1, blocking collectives, shards(): sum_all, sum_ref = lax.psum((sum_all, sum_ref), 'vocab')  128 us
    pmax x1, blocking collectives, shards(): peak_all, peak_ref = lax.pmax((peak_all, peak_ref), 'vocab')  125 us
    gather x3, local copies, waits for them, and re-layouts, shards(): picked = jnp.take_along_axis(logits, safe_ids, axis=1)  16.8 us
  transfers between devices with their start and end apart: 2, of which 2 were waited for; matrix products, arithmetic and copies ran while one was open for 1% of the time, Pallas kernels for 0%

commit v1 on v0

--- a/solution.py
+++ b/solution.py
@@ -7,6 +7,28 @@
 lowest = -1e30
 
 
+def laid_out(pieces, dim):
+    pieces = jnp.moveaxis(pieces, 0, dim)
+    shape = pieces.shape
+    return pieces.reshape(*shape[:dim], shape[dim] * shape[dim + 1], *shape[dim + 2 :])
+
+
+def gather_around(shard, axis, dim):
+    size = lax.axis_size(axis)
+    pairs = [(i, (i + 1) % size) for i in range(size)]
+    back = [(b, a) for a, b in pairs]
+    lower, upper = ([], [])
+    for step in range(size - 1):
+        if step % 2 == 0:
+            lower.append(lax.ppermute(lower[-1] if lower else shard, axis, pairs))
+        else:
+            upper.append(lax.ppermute(upper[-1] if upper else shard, axis, back))
+    blocks = jnp.stack([*lower[::-1], shard, *upper])
+    shift = lax.axis_index(axis) - len(lower)
+    blocks = blocks[(jnp.arange(size) - shift) % size]
+    return laid_out(blocks, dim)
+
+
 def shards(hidden, head, gain, refusal_ids, refusal_count, loss_scale):
     row_count, model_width = hidden.shape
     vocab_local = head.shape[1]
@@ -14,11 +36,7 @@
     hidden_f = hidden.astype(jnp.float32)
     inverse_rms = lax.rsqrt(jnp.mean(hidden_f * hidden_f, axis=1, keepdims=True) + epsilon)
     normed = (hidden_f * inverse_rms * gain).astype(jnp.bfloat16)
-    logits = jnp.dot(
-        normed,
-        lax.all_gather(head, "prompt", axis=0, tiled=True),
-        preferred_element_type=jnp.float32,
-    )
+    logits = jnp.dot(normed, gather_around(head, "prompt", 0), preferred_element_type=jnp.float32)
     vocab_start = lax.axis_index("vocab") * vocab_local
     shifted_ids = refusal_ids - vocab_start
     in_list = jnp.arange(list_length)[None, :] < refusal_count[:, None]

time: 739 us -> 933 us (1.26)
  waiting for transfers between devices: 292 us -> 437 us
  local copies, waits for them, and re-layouts: 17.6 us -> 40.6 us
  other arithmetic: 10.9 us -> 32.3 us
    ppermute x0 -> x3, waiting for transfers between devices: none -> 306 us  [the longest x2 306 us: gather_around(): lower.append(lax.ppermute(lower[-1] if lower else shard, axis, pairs))]
    all_gather x1, waiting for transfers between devices: 159 us -> 0.02 us  [shards(): lax.all_gather(head, 'prompt', axis=0, tiled=True)]
    gather x0 -> x4, local copies, waits for them, and re-layouts: none -> 22.8 us  [gather_around(): blocks = blocks[(jnp.arange(size) - shift) % size]]
  transfers between devices with their start and end apart: 2 -> 5, of which waited for: 2 -> 3; matrix products, arithmetic and copies ran while one was open for 1% -> 8% of each run, Pallas kernels for 0% -> 0%
where the time goes in v1:
time: 933 us; the launch traced here: 932 us
  waiting for transfers between devices  437 us (47%)
  blocking collectives  386 us (41%)
  local copies, waits for them, and re-layouts  40.6 us (4%)
  other arithmetic  32.3 us (3%)
  matrix products  15.9 us (2%)
  between operations  14.2 us (2%)
    ppermute x2, waiting for transfers between devices, gather_around(): lower.append(lax.ppermute(lower[-1] if lower else shard, axis, pairs))  306 us
    reduce_scatter x1, waiting for transfers between devices, shards(): lax.psum_scatter(grad_full, 'vocab', scatter_dimension=1, tiled=True)  130 us
    pmax x1, blocking collectives, shards(): peak_all, peak_ref = lax.pmax((peak_all, peak_ref), 'vocab')  130 us
    psum x1, blocking collectives, shards(): row_term = lax.psum(jnp.sum(grad_cols * normed_cols, axis=1), 'vocab')  129 us
    psum x1, blocking collectives, shards(): sum_all, sum_ref = lax.psum((sum_all, sum_ref), 'vocab')  127 us
    gather x4, local copies, waits for them, and re-layouts, gather_around(): blocks = blocks[(jnp.arange(size) - shift) % size]  22.8 us
  transfers between devices with their start and end apart: 5, of which 3 were waited for; matrix products, arithmetic and copies ran while one was open for 8% of the time, Pallas kernels for 0%

profile of v1, /device:TPU:1, one launch (start us, length us, event | category | flops | bytes accessed | tf_op | source)
XLA Modules:
  0.0 932.0 jit_solution(4105729861556939051)
XLA Ops:
  8.0 2.1 collective-permute-start
  10.1 1.4 collective-permute-start.2
  11.4 156.1 %collective-permute-done = bf16[2048,1024]{1,0:T(8,128)(2,1)} collective-permute-done((bf16[2048,1024]{1,0:T(8,128)(2,1)}, bf16[2048,1024]{1,0:T(8,128)(2,1)}, u32[]{:S(2)}, u32[]{:S(2)}) %collective-permute-start) | collective-permute-done | bytes 4194336 | tf_op jit(solution)/shard_map/ppermute | solution.py:23
  167.6 2.2 collective-permute-start.1
  170.7 2.3 multiply_reduce_fusion
  173.0 1.9 multiply_convert_fusion
  174.9 150.4 %collective-permute-done.1 = bf16[2048,1024]{1,0:T(8,128)(2,1)} collective-permute-done((bf16[2048,1024]{1,0:T(8,128)(2,1)}, bf16[2048,1024]{1,0:T(8,128)(2,1)}, u32[]{:S(2)}, u32[]{:S(2)}) %collective-permute-start.1) | collective-permute-done | bytes 4194336 | tf_op jit(solution)/shard_map/ppermute | solution.py:23
  325.3 7.3 pad_maximum_fusion
  332.6 5.0 fusion.14
  337.7 6.4 gather_fusion.1
  344.0 6.4 gather_fusion.2
  350.4 3.6 pad_maximum_fusion.2
  354.1 5.0 gather_fusion.3
  359.1 8.7 pad_maximum_fusion.1
  367.8 2.5 fusion.15
  370.3 16.6 %gather_fusion = f32[2048]{0:T(1024)S(1)} fusion(f32[128,1024]{1,0:T(8,128)S(1)} %get-tuple-element.18, s32[2048]{0:T(1024)S(1)} %reshape.92), kind=kCustom, calls=%fused_computation | custom fusion | bytes 32768 | tf_op jit(solution)/shard_map/jit(take_along_axis)/gather | solution.py:45
  387.2 129.6 %all-reduce.1 = (f32[128]{0:T(128)S(1)}, f32[128]{0:T(128)S(1)}) all-reduce(f32[128]{0:T(128)S(1)} %get-tuple-element.17, f32[128]{0:T(128)S(1)} %get-tuple-element.9), channel_id=1, replica_groups=mesh['prompt'=4,'vocab'=64] {'vocab'}, use_global_device_ids=true, to_apply=%region_7.8 | all-reduce | flops 256 | bytes 2048 | tf_op jit(solution)/shard_map/pmax | solution.py:48
  517.2 127.5 %all-reduce = (f32[128]{0:T(128)S(1)}, f32[128]{0:T(128)S(1)}) all-reduce(f32[128]{0:T(128)S(1)} %exponential_reduce_fusion, f32[128]{0:T(128)S(1)} %exponential_reduce_fusion.1), channel_id=1, replica_groups=mesh['prompt'=4,'vocab'=64] {'vocab'}, use_global_device_ids=true, to_apply=%region_9.10 | all-reduce | flops 256 | bytes 2048 | tf_op jit(solution)/shard_map/psum | solution.py:51
  645.2 2.4 fusion.1
  647.6 13.5 %fusion.2 = f32[128,8192]{1,0:T(8,128)} fusion(bf16[8192,1024]{1,0:T(8,128)(2,1)} %all-gather.2.cloned.1.call-done, f32[128,1024]{1,0:T(8,128)S(1)} %get-tuple-element.18, pred[128,1024]{1,0:T(8,128)(4,1)S(1)} %fusion.1, f32[128]{0:T(128)S(1)} %get-tuple-element.8, f32[128]{0:T(128)S(1)} %get-tuple-element.7, f32[128]{0:T(128)S(1)} %copy-done.4), kind=kOutput, calls=%fused_computation.14 | convolution fusion | flops 2148270080 | bytes 21628416 | tf_op jit(solution)/shard_map/dot_general | solution.py:66
  661.1 2.3 convert_element_type.12
  663.5 129.8 %reduce-scatter.2.cloned.1.call-done = f32[128,128]{1,0:T(8,128)} async-done(((f32[128,8192]{1,0:T(8,128)}), f32[128,128]{1,0:T(8,128)}) %reduce-scatter.2.cloned.1.call-update) | async-done | bytes 65552 | tf_op jit(solution)/shard_map/reduce_scatter | solution.py:72
  794.3 129.2 %psum.23 = f32[128]{0:T(128)S(1)} all-reduce(f32[128]{0:T(128)S(1)} %multiply_reduce_fusion.1), channel_id=1, replica_groups=mesh['prompt'=4,'vocab'=64] {'vocab'}, use_global_device_ids=true, to_apply=%region_12.13 | all-reduce | flops 128 | bytes 1024 | tf_op jit(solution)/shard_map/psum | solution.py:74
  923.5 1.6 multiply_subtract_fusion
  (31 shorter events, 4.0 us)
Async XLA Ops:
  7.2 165.9 %copy-start.1 = (bf16[128,8192]{1,0:T(8,128)(2,1)S(1)}, bf16[128,8192]{1,0:T(8,128)(2,1)}, u32[]{:S(2)}) copy-start(bf16[128,8192]{1,0:T(8,128)(2,1)} %param.6) | copy-start | bytes 6291460
  7.2 165.9 %copy-start.3 = (f32[8192]{0:T(1024)S(1)}, f32[8192]{0:T(1024)}, u32[]{:S(2)}) copy-start(f32[8192]{0:T(1024)} %param.8) | copy-start | bytes 98308
  7.2 640.4 %all-gather.2.cloned.1.call-start = ((), (), s32[]{:S(2)}) async-start(), calls=%async_computation.1 | async-start | bytes 20971520 | tf_op jit(solution)/shard_map/all_gather | solution.py:68
  7.9 785.4 %reduce-scatter.2.cloned.1.call-start = ((), (), s32[]{:S(2)}) async-start(), calls=%async_computation.2 | async-start | bytes 4259840 | tf_op jit(solution)/shard_map/reduce_scatter | solution.py:72
  8.0 159.6 %collective-permute-start = (bf16[2048,1024]{1,0:T(8,128)(2,1)}, bf16[2048,1024]{1,0:T(8,128)(2,1)}, u32[]{:S(2)}, u32[]{:S(2)}) collective-permute-start(bf16[2048,1024]{1,0:T(8,128)(2,1)} %param.7), channel_id=1, source_target_pairs={{0,64},{64,128},{128,192},{192,0},{1,65},{65,129},{129,193},{193,1... | collective-permute-start | bytes 12582920 | tf_op jit(solution)/shard_map/ppermute | solution.py:23
  10.1 164.9 %collective-permute-start.2 = (bf16[2048,1024]{1,0:T(8,128)(2,1)}, bf16[2048,1024]{1,0:T(8,128)(2,1)}, u32[]{:S(2)}, u32[]{:S(2)}) collective-permute-start(bf16[2048,1024]{1,0:T(8,128)(2,1)} %param.7), channel_id=1, source_target_pairs={{64,0},{128,64},{192,128},{0,192},{65,1},{129,65},{193,129},{1,193... | collective-permute-start | bytes 12582920 | tf_op jit(solution)/shard_map/ppermute | solution.py:25
  167.6 157.7 %collective-permute-start.1 = (bf16[2048,1024]{1,0:T(8,128)(2,1)}, bf16[2048,1024]{1,0:T(8,128)(2,1)}, u32[]{:S(2)}, u32[]{:S(2)}) collective-permute-start(bf16[2048,1024]{1,0:T(8,128)(2,1)} %collective-permute-done), channel_id=1, source_target_pairs={{0,64},{64,128},{128,192},{192,0},{1,65},{65,129},{129,193},{193,1... | collective-permute-start | bytes 12582920 | tf_op jit(solution)/shard_map/ppermute | solution.py:23
  170.7 154.6 %copy-start = (bf16[2048,1024]{1,0:T(8,128)(2,1)S(1)}, bf16[2048,1024]{1,0:T(8,128)(2,1)}, u32[]{:S(2)}) copy-start(bf16[2048,1024]{1,0:T(8,128)(2,1)} %param.7) | copy-start | bytes 12582916
  359.1 8.7 copy-start.2
  370.3 16.8 %copy-start.5 = (s32[128]{0:T(128)S(1)}, s32[128]{0:T(128)}, u32[]{:S(2)}) copy-start(s32[128]{0:T(128)} %param.10) | copy-start | bytes 1540
  370.3 277.4 %copy-start.4 = (f32[128]{0:T(128)S(1)}, f32[128]{0:T(128)}, u32[]{:S(2)}) copy-start(f32[128]{0:T(128)} %param.11) | copy-start | bytes 1540
Sparse Core Ops, SparseCore 0:
  9.8 290.0 all-gather.1
  661.2 132.0 reduce-scatter.1
